TPU v7x, 256 devices: a whole 4x4x8 slice. The times are simulated.
256 devices in a mesh: dp: 4 (over y), expert: 64 (over x, z, core).
Axes of the slice: x: 4, y: 4, z: 8, core: 2. Of those that a mesh axis runs over, the one named last changes fastest.
Arguments:
- tokens: bfloat16 [64, 88, 4096], P('expert'), may hold values from -6 to 6
- routing: int32 [64, 88, 8], P('expert'), may hold values from 0 to 63, as said below
- combine: float32 [64, 88, 8], P('expert'), may hold values from 0.05 to 0.5
- w_gate: bfloat16 [64, 4096, 1536], P('expert', None, 'dp'), may hold values from -0.09375 to 0.09375
- w_up: bfloat16 [64, 4096, 1536], P('expert', None, 'dp'), may hold values from -0.09375 to 0.09375
- w_down: bfloat16 [64, 1536, 4096], P('expert', 'dp'), may hold values from -0.15625 to 0.15625
Outputs:
- mixed: bfloat16 [64, 88, 4096], P('expert', None, 'dp')
Inputs may be any that keep to these rules, and one draw needn't show every extreme that they name: `routing`: each token names 8 different experts. In every group one expert, the same in all groups, is chosen by exactly 44 tokens; every other expert is chosen by 5 to 13 tokens of a group, and one of them, the same in all groups, by exactly 13 tokens of every group.
All inputs are finite; a program needn't handle non-finite values.
Results may differ from a plain program's by a relative error of at most 0.015.
Values may be sent and summed in bfloat16 or wider, within the bound.
A program may use at most 128 MiB of HBM per device.

v0:
```python
import jax
import jax.numpy as jnp
from jax import lax
from jax.sharding import PartitionSpec as P

CAP = 13
HOT_CAP = 44


def broadcast(block, axis, holder):
    block = jnp.where(lax.axis_index(axis) == holder, block, jnp.zeros_like(block))
    return lax.psum(block, axis)


def expert_partial(inputs, gate_mat, up_mat, down_mat):
    gate_val = jnp.dot(inputs, gate_mat, preferred_element_type=jnp.float32)
    up_val = jnp.dot(inputs, up_mat, preferred_element_type=jnp.float32)
    hidden = (jax.nn.silu(gate_val) * up_val).astype(jnp.bfloat16)
    return jnp.dot(hidden, down_mat, preferred_element_type=jnp.float32)


def local(tokens, routing, combine, w_gate, w_up, w_down):
    group_rows = tokens[0]
    chosen = routing[0]
    mixing = combine[0]
    owners = lax.axis_size("expert")
    local_experts = w_gate.shape[0]
    experts = owners * local_experts
    group_tok, top_k = chosen.shape
    model_width = group_rows.shape[1]
    capacity = CAP
    hot_capacity = HOT_CAP
    pick_ids = chosen.reshape(-1)
    one_hot = (pick_ids[:, None] == jnp.arange(experts, dtype=jnp.int32)[None, :]).astype(jnp.int32)
    counts = jnp.sum(one_hot, axis=0)
    hot_expert = jnp.argmax(counts)
    slot_rank = jnp.sum((jnp.cumsum(one_hot, axis=0) - 1) * one_hot, axis=1)
    is_hot = pick_ids == hot_expert
    token_of = jnp.arange(pick_ids.shape[0], dtype=jnp.int32) // top_k
    cold_slot = jnp.where(is_hot, experts * capacity, pick_ids * capacity + slot_rank)
    slot_token = (
        jnp.full((experts * capacity,), group_tok, jnp.int32)
        .at[cold_slot]
        .set(token_of, mode="drop")
    )
    hot_slot = jnp.where(is_hot, slot_rank, hot_capacity)
    hot_token = (
        jnp.full((hot_capacity,), group_tok, jnp.int32).at[hot_slot].set(token_of, mode="drop")
    )
    padded = jnp.concatenate([group_rows, jnp.zeros((1, model_width), group_rows.dtype)], axis=0)
    outgoing = jnp.take(padded, slot_token, axis=0).reshape(
        owners, local_experts, capacity, model_width
    )
    local_pick = hot_expert % local_experts
    owner_index = hot_expert // local_experts
    own_gate = lax.dynamic_index_in_dim(w_gate, local_pick, 0, keepdims=False)
    own_up = lax.dynamic_index_in_dim(w_up, local_pick, 0, keepdims=False)
    own_down = lax.dynamic_index_in_dim(w_down, local_pick, 0, keepdims=False)
    hot_gate, hot_up, hot_down = (
        broadcast(own_gate, "expert", owner_index),
        broadcast(own_up, "expert", owner_index),
        broadcast(own_down, "expert", owner_index),
    )
    hot_partial = expert_partial(jnp.take(padded, hot_token, axis=0), hot_gate, hot_up, hot_down)
    received = lax.all_to_all(outgoing, "expert", split_axis=0, concat_axis=0, tiled=True)
    gate_val = jnp.einsum("senm,emf->senf", received, w_gate, preferred_element_type=jnp.float32)
    up_val = jnp.einsum("senm,emf->senf", received, w_up, preferred_element_type=jnp.float32)
    hidden = (jax.nn.silu(gate_val) * up_val).astype(jnp.bfloat16)
    partial_value = jnp.einsum("senf,efm->senm", hidden, w_down, preferred_element_type=jnp.float32)
    returned = lax.all_to_all(
        partial_value.astype(jnp.bfloat16), "expert", split_axis=0, concat_axis=0, tiled=True
    )
    flat_back = returned.reshape(experts * capacity, returned.shape[3])
    cold_sum, hot_sum = (
        lax.psum_scatter(flat_back, "dp", scatter_dimension=1, tiled=True).astype(jnp.float32),
        lax.psum_scatter(
            hot_partial.astype(jnp.bfloat16), "dp", scatter_dimension=1, tiled=True
        ).astype(jnp.float32),
    )
    cold_share = cold_sum.astype(jnp.bfloat16)
    hot_share = hot_sum.astype(jnp.bfloat16)
    out_table = jnp.concatenate([cold_share, hot_share], axis=0)
    target = jnp.where(
        is_hot, experts * capacity + slot_rank, pick_ids * capacity + slot_rank
    ).reshape(group_tok, top_k)
    combined = jnp.zeros((group_tok, out_table.shape[1]), jnp.float32)
    for column in range(top_k):
        picked = jnp.take(out_table, target[:, column], axis=0).astype(jnp.float32)
        combined = combined + mixing[:, column : column + 1] * picked
    return combined.astype(jnp.bfloat16)[None]


def solution(mesh):
    placed = (
        P("expert", None, None),
        P("expert", None, None),
        P("expert", None, None),
        P("expert", None, "dp"),
        P("expert", None, "dp"),
        P("expert", "dp", None),
    )
    return jax.shard_map(
        local, mesh=mesh, in_specs=placed, out_specs=P("expert", None, "dp"), check_vma=False
    )
```

profile of v0, /device:TPU:1, one launch (start us, length us, event | category | flops | bytes accessed | tf_op | source)
XLA Modules:
  0.0 666.6 jit_solution(2950273191164341228)
XLA Ops:
  8.4 1.8 reduce-window.6
  12.2 4.1 scatter_custom_fusion
  16.5 1.2 concatenate.6
  17.7 6.5 gather_fusion
  24.2 9.1 %gather.14 = bf16[64,1,13,4096]{3,2,0,1:T(8,128)(2,1)} reshape(bf16[832,4096]{1,0:T(8,128)(2,1)} %gather_fusion) | data formatting | bytes 13631488 | tf_op jit(solution)/shard_map/jit(_take)/gather | solution.py:51
  33.3 7.4 %select_bitcast_fusion = bf16[64,1,13,4096]{3,2,1,0:T(8,128)(2,1)} fusion(bf16[64,1,13,4096]{3,2,0,1:T(8,128)(2,1)} %gather.14, pred[64,13]{1,0:T(8,128)(4,1)S(1)} %broadcast_in_dim.63), kind=kLoop, calls=%fused_computation.12 | loop fusion | flops 3407872 | bytes 13632320 | tf_op jit(solution)/shard_map/jit(_take)/select_n | solution.py:51
  40.8 199.3 %all_to_all.10 = bf16[64,1,13,4096]{3,2,1,0:T(8,128)(2,1)S(1)} all-to-all(bf16[64,1,13,4096]{3,2,1,0:T(8,128)(2,1)} %select_bitcast_fusion), channel_id=1, replica_groups=mesh['dp'=4,'expert'=64] {'expert'}, dimensions={0} | all-to-all | bytes 13631488 | tf_op jit(solution)/shard_map/all_to_all | solution.py:65
  240.1 4.4 fusion.10
  244.5 4.6 fusion.30
  249.1 5.6 fusion.4
  254.8 9.9 %copy.30 = bf16[64,1,13,4096]{3,2,1,0:T(8,128)(2,1)} copy(bf16[64,1,13,4096]{3,0,2,1:T(8,128)(2,1)} %fusion.4) | data formatting | bytes 13631488 | tf_op jit(solution)/shard_map/convert_element_type | solution.py:71
  264.7 6.0 all-to-all-start.1
  271.3 4.0 bitcast_select_fusion.1
  275.3 1.8 bitcast_select_fusion
  277.2 1.2 copy-done.4
  278.4 2.0 bitcast_select_fusion.2
  280.4 207.7 %all-to-all-done.1 = bf16[64,1,13,4096]{3,2,1,0:T(8,128)(2,1)} async-done(((bf16[64,1,13,4096]{3,2,1,0:T(8,128)(2,1)}), bf16[64,1,13,4096]{3,2,1,0:T(8,128)(2,1)}, u32[]{:S(2)}, u32[]{:S(2)}) %all-to-all-start.1) | async-done | bytes 6815776 | tf_op jit(solution)/shard_map/all_to_all | solution.py:70
  488.1 9.3 %reshape.144 = bf16[832,4096]{1,0:T(8,128)(2,1)} reshape(bf16[64,1,13,4096]{3,2,1,0:T(8,128)(2,1)} %all-to-all-done.1) | data formatting | bytes 13631488 | tf_op jit(solution)/shard_map/reshape | solution.py:73
  497.5 4.3 scatter_custom_fusion.1
  503.2 118.9 %all-reduce.5.cloned.1.call-done = (bf16[384,4096]{1,0:T(8,128)(2,1)}, bf16[4096,384]{1,0:T(8,128)(2,1)}, bf16[4096,384]{1,0:T(8,128)(2,1)}) async-done(((bf16[384,4096]{1,0:T(8,128)(2,1)}, bf16[4096,384]{1,0:T(8,128)(2,1)}, bf16[4096,384]{1,0:T(8,128)(2,1)}), (bf16[384,4096]{1,0:T(8,128)(2,1)}, bf16[4096,384]{1,0:T(8,128)(2,1)}, bf16[4096,384]{1,0:T(8,128)(2,1)})) %all-reduce.5.cloned.1.call-update) | async-done | bytes 9437200 | tf_op jit(solution)/shard_map/psum | solution.py:12
  622.1 2.5 fusion.39
  624.6 5.1 convolution_convert_fusion.1
  629.9 1.6 constant_dynamic-update-slice_fusion.1
  631.5 19.6 %reduce-scatter.5.cloned.1.call-done = bf16[44,1024]{1,0:T(8,128)(2,1)} async-done(((bf16[44,4096]{1,0:T(8,128)(2,1)}), bf16[44,1024]{1,0:T(8,128)(2,1)}) %reduce-scatter.5.cloned.1.call-update) | async-done | bytes 90128 | tf_op jit(solution)/shard_map/reduce_scatter | solution.py:76
  (70 shorter events, 12.8 us)
Async XLA Ops:
  40.8 199.3 %copy-start.3 = (bf16[1,4096,384]{2,1,0:T(8,128)(2,1)S(1)}, bf16[1,4096,384]{2,1,0:T(8,128)(2,1)}, u32[]{:S(2)}) copy-start(bf16[1,4096,384]{2,1,0:T(8,128)(2,1)} %param.11) | copy-start | bytes 9437188
  240.1 4.4 copy-start
  244.5 4.6 copy-start.1
  264.7 223.4 %all-to-all-start.1 = ((bf16[64,1,13,4096]{3,2,1,0:T(8,128)(2,1)}), bf16[64,1,13,4096]{3,2,1,0:T(8,128)(2,1)}, u32[]{:S(2)}, u32[]{:S(2)}) async-start(bf16[64,1,13,4096]{3,2,1,0:T(8,128)(2,1)} %copy.30), calls=%async_computation.1 | async-start | bytes 16777216 | tf_op jit(solution)/shard_map/all_to_all | solution.py:70
  270.7 351.4 %all-reduce.5.cloned.1.call-start = ((), (), s32[]{:S(2)}) async-start(), calls=%async_computation.6 | async-start | bytes 18874368 | tf_op jit(solution)/shard_map/psum | solution.py:12
  271.3 4.0 copy-start.2
  275.3 3.0 copy-start.4
  280.3 349.5 %reduce-scatter.3.cloned.1.call-start = ((), (), s32[]{:S(2)}) async-start(), calls=%async_computation.4 | async-start | bytes 8519680 | tf_op jit(solution)/shard_map/reduce_scatter | solution.py:75
  497.4 153.6 %reduce-scatter.5.cloned.1.call-start = ((), (), s32[]{:S(2)}) async-start(), calls=%async_computation.5 | async-start | bytes 491520 | tf_op jit(solution)/shard_map/reduce_scatter | solution.py:76
  624.6 5.2 copy-start.5
Sparse Core Ops, SparseCore 0:
  280.5 341.5 all-reduce.4
Sparse Core Ops, SparseCore 1:
  497.5 67.2 reduce-scatter.2
  629.8 21.1 reduce-scatter.4
where the time goes:
time: 669 us; the launch traced here: 667 us
  waiting for transfers between devices  346 us (52%)
  blocking collectives  199 us (30%)
  local copies, waits for them, and re-layouts  57 us (9%)
  matrix products  22.3 us (3%)
  other arithmetic  19.9 us (3%)
  between operations  15.8 us (2%)
    all_to_all x1, waiting for transfers between devices, local(): lax.all_to_all(partial_value.astype(jnp.bfloat16), 'expert', split_axis=0...  208 us
    all_to_all x1, blocking collectives, local(): lax.all_to_all(outgoing, 'expert', split_axis=0, concat_axis=0, tiled=True)  199 us
    psum x1, waiting for transfers between devices, broadcast(): return lax.psum(block, axis)  119 us
    reduce_scatter x1, waiting for transfers between devices, local(): lax.psum_scatter(hot_partial.astype(jnp.bfloat16), 'dp', scatter_dimensio...  19.6 us
    gather x2, local copies, waits for them, and re-layouts, local(): jnp.take(padded, slot_token, axis=0)  15.6 us
  transfers between devices with their start and end apart: 4, of which 3 were waited for; matrix products, arithmetic and copies ran while one was open for 5% of the time, Pallas kernels for 0%

commit v1 on v0

v1 whole, which is shorter than its diff:
```python
import functools

import jax
import jax.numpy as jnp
import numpy as np
from jax import lax
from jax.experimental import pallas as pl
from jax.experimental.pallas import tpu as pltpu
from jax.sharding import PartitionSpec as P

CAP = 13
HOT_CAP = 44
SLOT = 16
BLOCKS = 4
MESH = pl.DeviceIdType.MESH
VMEM = pltpu.VMEM
BF16 = jnp.bfloat16
F32 = jnp.float32


def dot(a, b):
    return jnp.dot(a, b, preferred_element_type=F32)


def cold_kernel(
    tok, pick, mix_hi, mix_lo, pack, unpack, gate_hbm, up_hbm, down_hbm, out,
    sent, got, rows, part, relay_up, relay_down, from_up, from_down, spread, back,
    w_gate, w_up, w_down, acc_gate, acc_up,
    load_sem, disp_send, disp_recv, y_send, y_recv, back_send, back_recv,
):
    n_dp, experts = rows.shape[0], got.shape[0] // SLOT
    per = experts // BLOCKS
    padded, packed = per * SLOT, per * CAP
    quarter = sent.shape[1]
    half = quarter // 2
    me, mine = lax.axis_index("dp"), lax.axis_index("expert")
    my_block, my_place = mine // per, mine % per
    above, below, across = (me + 1) % n_dp, (me + n_dp - 1) % n_dp, (me + 2) % n_dp

    loads = [
        pltpu.make_async_copy(src, dst, load_sem.at[i])
        for i, (src, dst) in enumerate(((gate_hbm, w_gate), (up_hbm, w_up), (down_hbm, w_down)))
    ]
    for load in loads:
        load.start()

    own_cols = pl.ds(pl.multiple_of(me * quarter, 128), quarter)

    @pl.loop(0, BLOCKS)
    def _(b):
        at = pl.ds(pl.multiple_of(b * padded, padded), padded)
        sent[at, :] = dot(pick[at, :], tok[:, own_cols]).astype(BF16)

    def slot(i):
        return pl.ds(pl.multiple_of(i * SLOT, SLOT), SLOT)

    own = slot(mine)
    got[own, :] = sent[own, :]

    def exchange(src, dst, to, send_sem, recv_sem):
        return pltpu.make_async_remote_copy(
            src_ref=src.at[slot(to), :], dst_ref=dst.at[own, :], send_sem=send_sem, recv_sem=recv_sem,
            device_id={"expert": to}, device_id_type=MESH,
        )

    for j in range(BLOCKS):

        @pl.loop(1 if j == 0 else 0, per)
        def _(i, j=j):
            to = ((my_block + j) % BLOCKS) * per + (my_place + i) % per
            exchange(sent, got, to, disp_send, disp_recv.at[j]).start()

    def across_dp(kind, j, src, dst, to):
        return pltpu.make_async_remote_copy(
            src_ref=src, dst_ref=dst, send_sem=y_send.at[kind, j], recv_sem=y_recv.at[kind, j],
            device_id={"dp": to}, device_id_type=MESH,
        )

    def block_of(j):
        return (my_block + BLOCKS - j) % BLOCKS

    def packed_at(j):
        return pl.ds(pl.multiple_of(block_of(j) * packed, 16), packed)

    def padded_at(j):
        return pl.ds(pl.multiple_of(block_of(j) * padded, padded), padded)

    left, right = pl.ds(0, half), pl.ds(half, half)
    copies = {}

    def start(kind, j, src, dst, to):
        copies[kind, j] = across_dp(kind, j, src, dst, to)
        copies[kind, j].start()

    def gather_rows(j):
        take = per - 1 if j == 0 else per
        pltpu.make_async_copy(
            got.at[pl.ds(0, take * SLOT), :], got.at[pl.ds(0, take * SLOT), :], disp_recv.at[j]
        ).wait()
        at = packed_at(j)
        rows[me, at, :] = dot(pack[...], got[padded_at(j), :]).astype(BF16)
        start(0, j, rows.at[me, at, :], rows.at[me, at, :], above)
        start(1, j, rows.at[me, at, :], rows.at[me, at, :], below)

    def forward_rows(j):
        at = packed_at(j)
        copies[0, j].wait_recv()
        start(2, j, rows.at[below, at, left], rows.at[below, at, left], above)
        copies[1, j].wait_recv()
        start(3, j, rows.at[above, at, right], rows.at[above, at, right], below)

    def compute(j):
        at = packed_at(j)
        copies[2, j].wait_recv()
        copies[3, j].wait_recv()
        acc_gate[...] = jnp.zeros_like(acc_gate)
        acc_up[...] = jnp.zeros_like(acc_up)

        @pl.loop(0, n_dp)
        def _(q):
            depth = pl.ds(pl.multiple_of(q * quarter, quarter), quarter)
            acc_gate[...] += dot(rows[q, at, :], w_gate[depth, :])
            acc_up[...] += dot(rows[q, at, :], w_up[depth, :])

        hidden = (jax.nn.silu(acc_gate[...]) * acc_up[...]).astype(BF16)

        @pl.loop(0, n_dp)
        def _(i):
            q = (across + i) % n_dp
            cols = pl.ds(pl.multiple_of(q * quarter, quarter), quarter)
            part[q, at, :] = dot(hidden, w_down[:, cols]).astype(BF16)

        start(4, j, part.at[across, at, left], relay_up.at[at, :], above)
        start(5, j, part.at[across, at, right], relay_down.at[at, :], below)

    def relay(j):
        at = packed_at(j)
        copies[4, j].wait_recv()
        part[above, at, left] = (part[above, at, left].astype(F32) + relay_up[at, :].astype(F32)).astype(BF16)
        start(6, j, part.at[above, at, :], from_down.at[at, :], above)
        copies[5, j].wait_recv()
        part[below, at, right] = (part[below, at, right].astype(F32) + relay_down[at, :].astype(F32)).astype(BF16)
        start(7, j, part.at[below, at, :], from_up.at[at, :], below)

    def send_back(j):
        at, wide = packed_at(j), padded_at(j)
        copies[6, j].wait_recv()
        copies[7, j].wait_recv()
        total = part[me, at, :].astype(F32) + from_down[at, :].astype(F32) + from_up[at, :].astype(F32)
        spread[wide, :] = dot(unpack[...], total.astype(BF16)).astype(BF16)
        if j == 0:
            back[own, :] = spread[own, :]

        @pl.loop(1 if j == 0 else 0, per)
        def _(i):
            to = block_of(j) * per + (my_place + i) % per
            exchange(spread, back, to, back_send, back_recv).start()

    stages = (gather_rows, forward_rows, compute, relay, send_back)
    delays = (0, 1, 2, 3, 4)
    for step in range(BLOCKS + delays[-1]):
        for stage, delay in zip(stages, delays):
            j = step - delay
            if 0 <= j < BLOCKS:
                if stage is compute and j == 0:
                    for load in loads:
                        load.wait()
                stage(j)

    others = pl.ds(0, (experts - 1) * SLOT)
    pltpu.make_async_copy(back.at[others, :], back.at[others, :], back_recv).wait()
    down_rows = (((0,), (0,)), ((), ()))
    mixed = lax.dot_general(mix_hi[...], back[...], down_rows, preferred_element_type=F32)
    out[...] = mixed + lax.dot_general(mix_lo[...], back[...], down_rows, preferred_element_type=F32)

    pltpu.make_async_copy(sent.at[others, :], sent.at[others, :], disp_send).wait()
    pltpu.make_async_copy(spread.at[others, :], spread.at[others, :], back_send).wait()
    for copy in copies.values():
        copy.wait_send()


def cold_experts(tokens, pick, mix_hi, mix_lo, w_gate, w_up, w_down):
    group_tok, width = tokens.shape
    experts, n_dp = lax.axis_size("expert"), lax.axis_size("dp")
    units, quarter, per = w_gate.shape[1], width // n_dp, experts // BLOCKS
    slots, held = experts * SLOT, experts * CAP
    block = per * CAP
    place = np.arange(block)
    wanted = (place // CAP) * SLOT + place % CAP
    pack = jnp.asarray(wanted[:, None] == np.arange(per * SLOT)[None, :], BF16)
    unpack = jnp.asarray(wanted[None, :] == np.arange(per * SLOT)[:, None], BF16)
    vmem, anywhere = pl.BlockSpec(memory_space=VMEM), pl.BlockSpec(memory_space=pl.ANY)
    dma = pltpu.SemaphoreType.DMA
    return pl.pallas_call(
        cold_kernel,
        name="cold_experts",
        out_shape=jax.ShapeDtypeStruct((group_tok, quarter), F32),
        in_specs=[vmem] * 6 + [anywhere] * 3,
        out_specs=vmem,
        scratch_shapes=[
            VMEM((slots, quarter), BF16),
            VMEM((slots, quarter), BF16),
            VMEM((n_dp, held, quarter), BF16),
            VMEM((n_dp, held, quarter), BF16),
            VMEM((held, quarter // 2), BF16),
            VMEM((held, quarter // 2), BF16),
            VMEM((held, quarter), BF16),
            VMEM((held, quarter), BF16),
            VMEM((slots, quarter), BF16),
            VMEM((slots, quarter), BF16),
            VMEM((width, units), BF16),
            VMEM((width, units), BF16),
            VMEM((units, width), BF16),
            VMEM((block, units), F32),
            VMEM((block, units), F32),
            dma((3,)),
            dma,
            dma((BLOCKS,)),
            dma((8, BLOCKS)),
            dma((8, BLOCKS)),
            dma,
            dma,
        ],
        compiler_params=pltpu.CompilerParams(vmem_limit_bytes=56 << 20, has_side_effects=True),
        cost_estimate=pl.CostEstimate(
            flops=6 * held * width * units, bytes_accessed=60 << 20, transcendentals=held * units
        ),
    )(tokens, pick, mix_hi, mix_lo, pack, unpack, w_gate, w_up, w_down)


def expert_partial(inputs, gate_mat, up_mat, down_mat):
    gate_val = jnp.dot(inputs, gate_mat, preferred_element_type=F32)
    up_val = jnp.dot(inputs, up_mat, preferred_element_type=F32)
    hidden = (jax.nn.silu(gate_val) * up_val).astype(BF16)
    return jnp.dot(hidden, down_mat, preferred_element_type=F32)


def split_weight(weight):
    high = lax.reduce_precision(weight, 8, 7)
    return high.astype(BF16), (weight - high).astype(BF16)


def local(tokens, routing, combine, w_gate, w_up, w_down):
    group_rows, chosen, mixing = tokens[0], routing[0], combine[0]
    w_gate, w_up, w_down = w_gate[0], w_up[0], w_down[0]
    group_tok = chosen.shape[0]
    experts = lax.axis_size("expert")
    ids = jnp.arange(experts, dtype=jnp.int32)
    hit = chosen.T[None, :, :] == ids[:, None, None]
    member = jnp.sum(hit.astype(F32), axis=1)
    weight = jnp.sum(jnp.where(hit, mixing.T[None, :, :], 0.0), axis=1)
    earlier = jnp.asarray(np.triu(np.ones((group_tok, group_tok)), 1), BF16)
    before = jnp.dot(member.astype(BF16), earlier, preferred_element_type=F32)
    hot_expert = jnp.argmax(jnp.sum(member, axis=1)).astype(jnp.int32)
    is_hot = (ids == hot_expert)[:, None]
    rank = jnp.where(member > 0, before, -1.0)

    picked = jnp.where(is_hot, -1.0, rank)[:, None, :] == jnp.arange(SLOT, dtype=F32)[None, :, None]
    high, low = split_weight(weight)
    zero = jnp.zeros((), BF16)
    pick = picked.astype(BF16).reshape(experts * SLOT, group_tok)
    mix_hi = jnp.where(picked, high[:, None, :], zero).reshape(experts * SLOT, group_tok)
    mix_lo = jnp.where(picked, low[:, None, :], zero).reshape(experts * SLOT, group_tok)

    hot_rank = jnp.sum(jnp.where(is_hot, rank, 0.0), axis=0)
    hot_weight = jnp.sum(jnp.where(is_hot, weight, 0.0), axis=0)
    hot_pick = hot_rank[None, :] == jnp.arange(HOT_CAP, dtype=F32)[:, None]

    owned = lax.axis_index("expert") == hot_expert
    hot_gate, hot_up, hot_down = lax.psum(
        tuple(jnp.where(owned, w, jnp.zeros_like(w)) for w in (w_gate, w_up, w_down)), "expert"
    )
    cold = cold_experts(group_rows, pick, mix_hi, mix_lo, w_gate, w_up, w_down)
    hot_rows = jnp.dot(hot_pick.astype(BF16), group_rows, preferred_element_type=F32).astype(BF16)
    hot_part = expert_partial(hot_rows, hot_gate, hot_up, hot_down)
    hot_sum = lax.psum_scatter(hot_part.astype(BF16), "dp", scatter_dimension=1, tiled=True)
    hot_mix = jnp.where(hot_pick, hot_weight[None, :], 0.0)
    hot = lax.dot_general(
        hot_mix, hot_sum.astype(F32), (((0,), (0,)), ((), ())),
        precision=lax.Precision.HIGHEST, preferred_element_type=F32,
    )
    return (cold + hot).astype(BF16)[None]


def solution(mesh):
    placed = (
        P("expert", None, None),
        P("expert", None, None),
        P("expert", None, None),
        P("expert", None, "dp"),
        P("expert", None, "dp"),
        P("expert", "dp", None),
    )
    return jax.shard_map(
        local, mesh=mesh, in_specs=placed, out_specs=P("expert", None, "dp"), check_vma=False
    )
```

time: 669 us -> 411 us (0.61)
  blocking collectives: 199 us -> 0 us
  Pallas kernels: 0 us -> 167 us
  waiting for transfers between devices: 346 us -> 207 us
  local copies, waits for them, and re-layouts: 57 us -> 1.14 us
  matrix products: 22.3 us -> 9.8 us
  other arithmetic: 19.9 us -> 11.6 us
    all_to_all x1 -> x0, waiting for transfers between devices: 208 us -> none  [local(): lax.all_to_all(partial_value.astype(jnp.bfloat16), 'expert', split_axis=0...]
    all_to_all x1 -> x0, blocking collectives: 199 us -> none  [local(): lax.all_to_all(outgoing, 'expert', split_axis=0, concat_axis=0, tiled=True)]
    pallas_call x0 -> x1, Pallas kernels: none -> 167 us  [cold_experts(): pl.pallas_call(cold_kernel, name='cold_experts', out_shape=jax.ShapeDtype...]
    psum x1, waiting for transfers between devices: 119 us -> 207 us  [local(): lax.psum(tuple((jnp.where(owned, w, jnp.zeros_like(w)) for w in (w_gate,...]
    gather x11 -> x0, local copies, waits for them, and re-layouts: 22.5 us -> none  [the longest x2 15.6 us: local(): jnp.take(padded, slot_token, axis=0)]
    reduce_scatter x2 -> x1, waiting for transfers between devices: 19.6 us -> 0.02 us  [local(): lax.psum_scatter(hot_part.astype(BF16), 'dp', scatter_dimension=1, tiled=...]
    dot_general x5, matrix products: 22.3 us -> 9.8 us  [the longest x1 4.07 us: expert_partial(): return jnp.dot(hidden, down_mat, preferred_element_type=F32)]
    convert_element_type x1 -> x0, local copies, waits for them, and re-layouts: 9.94 us -> none  [local(): partial_value.astype(jnp.bfloat16)]
  transfers between devices with their start and end apart: 4 -> 2, of which waited for: 3 -> 1; matrix products, arithmetic and copies ran while one was open for 5% -> 1% of each run, Pallas kernels for 0% -> 41%
where the time goes in v1:
time: 411 us; the launch traced here: 410 us
  waiting for transfers between devices  207 us (50%)
  Pallas kernels  167 us (41%)
  between operations  14.1 us (3%)
  other arithmetic  11.6 us (3%)
  matrix products  9.8 us (2%)
    psum x1, waiting for transfers between devices, local(): lax.psum(tuple((jnp.where(owned, w, jnp.zeros_like(w)) for w in (w_gate,...  207 us
    pallas_call x1, Pallas kernels, cold_experts(): pl.pallas_call(cold_kernel, name='cold_experts', out_shape=jax.ShapeDtype...  167 us
  transfers between devices with their start and end apart: 2, of which 1 were waited for; matrix products, arithmetic and copies ran while one was open for 1% of the time, Pallas kernels for 41%

profile of v1, /device:TPU:1, one launch (start us, length us, event | category | flops | bytes accessed | tf_op | source)
XLA Modules:
  0.0 410.4 jit_solution(2437131718368497474)
XLA Ops:
  6.5 1.3 select_reduce_fusion
  7.8 0.7 iota_reduce_fusion
  9.1 0.0 copy-start.1
  9.1 0.0 copy-start.2
  9.1 3.9 broadcast_select_fusion
  13.0 0.0 copy-done.1
  13.0 1.0 copy-done.2
  14.0 3.2 broadcast_select_fusion.1
  17.3 0.0 all-reduce.3.cloned.1.call-update
  17.3 0.0 reduce-scatter.2.cloned.1.call-start
  17.3 0.1 eq.71
  17.4 0.7 iota_compare_fusion.4
  18.1 0.0 copy-done.4
  18.1 0.2 select_reduce_fusion.1
  18.3 0.9 fusion.5.pick
  19.2 1.0 fusion.3
  20.2 0.3 convolution_convert_fusion.1
  20.5 207.1 %all-reduce.3.cloned.1.call-done = (bf16[384,4096]{1,0:T(8,128)(2,1)}, bf16[4096,384]{1,0:T(8,128)(2,1)}, bf16[4096,384]{1,0:T(8,128)(2,1)}) async-done(((bf16[384,4096]{1,0:T(8,128)(2,1)}, bf16[4096,384]{1,0:T(8,128)(2,1)}, bf16[4096,384]{1,0:T(8,128)(2,1)}), (bf16[384,4096]{1,0:T(8,128)(2,1)}, bf16[4096,384]{1,0:T(8,128)(2,1)}, bf16[4096,384]{1,0:T(8,128)(2,1)})) %all-reduce.3.cloned.1.call-update) | async-done | bytes 9437200 | tf_op jit(solution)/shard_map/psum | solution.py:270
  227.6 3.2 fusion.22
  230.8 4.1 convolution_convert_fusion
  234.9 0.0 reduce-scatter.2.cloned.1.call-update
  234.9 166.5 %cold_experts.1 = f32[88,1024]{1,0:T(8,128)} custom-call(bf16[88,4096]{1,0:T(8,128)(2,1)} %bitcast.39, bf16[1024,88]{1,0:T(8,128)(2,1)} %fusion.5.pick, bf16[1024,88]{1,0:T(8,128)(2,1)} %get-tuple-element.16.mix_hi, bf16[1024,88]{1,0:T(8,128)(2,1)} %get-tuple-element.15.mix_lo, bf16[208,256]{1,0:T(8,128)(2,1)} %constant.29.clone.pack, ...), custom_call_target="tpu_custom_call" | custom-call | flops 7851737088 | bytes 62914560 | tf_op jit(solution)/shard_map/cold_experts/pallas_call | solution.py:194
  401.4 0.0 reduce-scatter.2.cloned.1.call-done
  401.5 2.1 fusion.1
  (7 shorter events, 0.0 us)
Async XLA Ops:
  6.5 221.0 %all-reduce.3.cloned.1.call-start = ((), (), s32[]{:S(2)}) async-start(), calls=%async_computation.2 | async-start | bytes 18874368 | tf_op jit(solution)/shard_map/psum | solution.py:270
  9.1 3.9 copy-start.1
  9.1 4.9 %copy-start.2 = (bf16[1,4096,384]{2,1,0:T(8,128)(2,1)S(1)}, bf16[1,4096,384]{2,1,0:T(8,128)(2,1)}, u32[]{:S(2)}) copy-start(bf16[1,4096,384]{2,1,0:T(8,128)(2,1)} %param.13) | copy-start | bytes 9437188
  17.3 0.9 copy-start.4
  17.3 2.9 copy-start.3
  17.3 384.2 %reduce-scatter.2.cloned.1.call-start = ((), (), s32[]{:S(2)}) async-start(), calls=%async_computation.1 | async-start | bytes 491520 | tf_op jit(solution)/shard_map/reduce_scatter | solution.py:276
  227.6 3.2 copy-start
Sparse Core Ops, SparseCore 0:
  17.4 210.1 all-reduce.2
  235.0 21.7 reduce-scatter.1

commit v2 on v1

--- a/solution.py
+++ b/solution.py
@@ -271,6 +271,7 @@
         tuple(jnp.where(owned, w, jnp.zeros_like(w)) for w in (w_gate, w_up, w_down)), "expert"
     )
     cold = cold_experts(group_rows, pick, mix_hi, mix_lo, w_gate, w_up, w_down)
+    hot_pick, cold = lax.optimization_barrier((hot_pick, cold))
     hot_rows = jnp.dot(hot_pick.astype(BF16), group_rows, preferred_element_type=F32).astype(BF16)
     hot_part = expert_partial(hot_rows, hot_gate, hot_up, hot_down)
     hot_sum = lax.psum_scatter(hot_part.astype(BF16), "dp", scatter_dimension=1, tiled=True)

time: 411 us -> 315 us (0.77)
  waiting for transfers between devices: 207 us -> 98.8 us
  Pallas kernels: 167 us -> 178 us
    psum x1, waiting for transfers between devices: 207 us -> 77.3 us  [local(): lax.psum(tuple((jnp.where(owned, w, jnp.zeros_like(w)) for w in (w_gate,...]
    reduce_scatter x1, waiting for transfers between devices: 0.02 us -> 21.5 us  [local(): lax.psum_scatter(hot_part.astype(BF16), 'dp', scatter_dimension=1, tiled=...]
    pallas_call x1, Pallas kernels: 167 us -> 178 us  [cold_experts(): pl.pallas_call(cold_kernel, name='cold_experts', out_shape=jax.ShapeDtype...]
  transfers between devices with their start and end apart: 2 -> 2, of which waited for: 1 -> 2; matrix products, arithmetic and copies ran while one was open for 1% -> 1% of each run, Pallas kernels for 41% -> 57%
where the time goes in v2:
time: 315 us; the launch traced here: 314 us
  Pallas kernels  178 us (57%)
  waiting for transfers between devices  98.8 us (31%)
  between operations  14.1 us (4%)
  other arithmetic  11.6 us (4%)
  matrix products  9.79 us (3%)
    pallas_call x1, Pallas kernels, cold_experts(): pl.pallas_call(cold_kernel, name='cold_experts', out_shape=jax.ShapeDtype...  178 us
    psum x1, waiting for transfers between devices, local(): lax.psum(tuple((jnp.where(owned, w, jnp.zeros_like(w)) for w in (w_gate,...  77.3 us
    reduce_scatter x1, waiting for transfers between devices, local(): lax.psum_scatter(hot_part.astype(BF16), 'dp', scatter_dimension=1, tiled=...  21.5 us
    select_n x2, other arithmetic, local(): jnp.where(owned, w, jnp.zeros_like(w))  7.09 us
  transfers between devices with their start and end apart: 2, of which 2 were waited for; matrix products, arithmetic and copies ran while one was open for 1% of the time, Pallas kernels for 57%

profile of v2, /device:TPU:1, one launch (start us, length us, event | category | flops | bytes accessed | tf_op | source)
XLA Modules:
  0.0 313.9 jit_solution(212214165644483021)
XLA Ops:
  6.5 1.3 select_reduce_fusion
  7.8 0.7 iota_reduce_fusion
  9.1 0.0 copy-start.1
  9.1 0.0 copy-start.2
  9.1 3.9 %broadcast_select_fusion = bf16[384,4096]{1,0:T(8,128)(2,1)} fusion(pred[]{:T(512)S(6)} %eq.77, bf16[1,384,4096]{2,1,0:T(8,128)(2,1)} %param.14), kind=kLoop, calls=%fused_computation.2 | loop fusion | flops 1572864 | bytes 6291457 | tf_op jit(solution)/shard_map/jit(_where)/select_n | solution.py:271
  13.0 0.0 copy-done.1
  13.0 1.0 copy-done.2
  14.0 3.2 %broadcast_select_fusion.1 = (bf16[4096,384]{1,0:T(8,128)(2,1)}, bf16[4096,384]{1,0:T(8,128)(2,1)}) fusion(pred[]{:T(512)S(6)} %eq.77, bf16[1,4096,384]{2,1,0:T(8,128)(2,1)S(1)} %copy-done.2, bf16[1,4096,384]{2,1,0:T(8,128)(2,1)S(1)} %copy-done.1), kind=kLoop, calls=%fused_computation.3 | loop fusion | flops 3145728 | bytes 12582913 | tf_op jit(solution)/shard_map/jit(_where)/select_n | solution.py:271
  17.3 0.0 all-reduce.3.cloned.1.call-update
  17.3 0.0 reduce-scatter.2.cloned.1.call-start
  17.3 0.1 eq.74
  17.4 0.6 iota_compare_fusion.2
  18.1 0.2 select_reduce_fusion.1
  18.2 0.9 fusion.5.pick
  19.1 1.0 fusion.3
  20.1 0.0 copy-start.3
  20.2 178.4 %cold_experts.1 = f32[88,1024]{1,0:T(8,128)} custom-call(bf16[88,4096]{1,0:T(8,128)(2,1)} %bitcast.40, bf16[1024,88]{1,0:T(8,128)(2,1)} %fusion.5.pick, bf16[1024,88]{1,0:T(8,128)(2,1)} %get-tuple-element.20.mix_hi, bf16[1024,88]{1,0:T(8,128)(2,1)} %get-tuple-element.19.mix_lo, bf16[208,256]{1,0:T(8,128)(2,1)} %constant.29.clone.pack, ...), custom_call_target="tpu_custom_call" | custom-call | flops 7851737088 | bytes 62914560 | tf_op jit(solution)/shard_map/cold_experts/pallas_call | solution.py:194
  198.5 0.3 convolution_convert_fusion.1
  198.8 77.3 %all-reduce.3.cloned.1.call-done = (bf16[384,4096]{1,0:T(8,128)(2,1)}, bf16[4096,384]{1,0:T(8,128)(2,1)}, bf16[4096,384]{1,0:T(8,128)(2,1)}) async-done(((bf16[384,4096]{1,0:T(8,128)(2,1)}, bf16[4096,384]{1,0:T(8,128)(2,1)}, bf16[4096,384]{1,0:T(8,128)(2,1)}), (bf16[384,4096]{1,0:T(8,128)(2,1)}, bf16[4096,384]{1,0:T(8,128)(2,1)}, bf16[4096,384]{1,0:T(8,128)(2,1)})) %all-reduce.3.cloned.1.call-update) | async-done | bytes 9437200 | tf_op jit(solution)/shard_map/psum | solution.py:270
  276.1 3.2 %fusion.20 = f32[44,384]{1,0:T(8,128)} fusion(bf16[44,4096]{1,0:T(8,128)(2,1)S(1)} %convolution_convert_fusion.1, bf16[4096,384]{1,0:T(8,128)(2,1)} %get-tuple-element.18), kind=kOutput, calls=%fused_computation.41 | convolution fusion | flops 138412032 | bytes 3573760 | tf_op jit(solution)/shard_map/dot_general | solution.py:232
  279.3 4.1 %convolution_convert_fusion = bf16[44,4096]{1,0:T(8,128)(2,1)} fusion(bf16[384,4096]{1,0:T(8,128)(2,1)S(1)} %copy-done, bf16[44,4096]{1,0:T(8,128)(2,1)S(1)} %convolution_convert_fusion.1, bf16[4096,384]{1,0:T(8,128)(2,1)} %get-tuple-element.17, f32[44,384]{1,0:T(8,128)} %fusion.20), kind=kOutput, calls=%fused_computation | convolution fusion | flops 277105664 | bytes 7079936 | tf_op jit(solution)/shard_map/dot_general | solution.py:235
  283.4 0.0 reduce-scatter.2.cloned.1.call-update
  283.4 21.5 %reduce-scatter.2.cloned.1.call-done = bf16[44,1024]{1,0:T(8,128)(2,1)} async-done(((bf16[44,4096]{1,0:T(8,128)(2,1)}), bf16[44,1024]{1,0:T(8,128)(2,1)}) %reduce-scatter.2.cloned.1.call-update) | async-done | bytes 90128 | tf_op jit(solution)/shard_map/reduce_scatter | solution.py:277
  305.0 2.1 fusion.1
  (8 shorter events, 0.0 us)
Async XLA Ops:
  6.5 269.6 %all-reduce.3.cloned.1.call-start = ((), (), s32[]{:S(2)}) async-start(), calls=%async_computation.2 | async-start | bytes 18874368 | tf_op jit(solution)/shard_map/psum | solution.py:270
  9.1 3.9 %copy-start.1 = (bf16[1,4096,384]{2,1,0:T(8,128)(2,1)S(1)}, bf16[1,4096,384]{2,1,0:T(8,128)(2,1)}, u32[]{:S(2)}) copy-start(bf16[1,4096,384]{2,1,0:T(8,128)(2,1)} %param.12) | copy-start | bytes 9437188
  9.1 4.9 %copy-start.2 = (bf16[1,4096,384]{2,1,0:T(8,128)(2,1)S(1)}, bf16[1,4096,384]{2,1,0:T(8,128)(2,1)}, u32[]{:S(2)}) copy-start(bf16[1,4096,384]{2,1,0:T(8,128)(2,1)} %param.13) | copy-start | bytes 9437188
  17.3 0.8 copy-start.4
  17.3 287.7 %reduce-scatter.2.cloned.1.call-start = ((), (), s32[]{:S(2)}) async-start(), calls=%async_computation.1 | async-start | bytes 491520 | tf_op jit(solution)/shard_map/reduce_scatter | solution.py:277
  20.1 178.4 %copy-start.3 = (bf16[1,88,4096]{2,1,0:T(8,128)(2,1)S(1)}, bf16[1,88,4096]{2,1,0:T(8,128)(2,1)}, u32[]{:S(2)}) copy-start(bf16[1,88,4096]{2,1,0:T(8,128)(2,1)} %param.9) | copy-start | bytes 2162692
  276.1 3.2 %copy-start = (bf16[384,4096]{1,0:T(8,128)(2,1)S(1)}, bf16[384,4096]{1,0:T(8,128)(2,1)}, u32[]{:S(2)}) copy-start(bf16[384,4096]{1,0:T(8,128)(2,1)} %get-tuple-element.16) | copy-start | bytes 9437188
Sparse Core Ops, SparseCore 0:
  17.4 258.6 all-reduce.2
  283.6 21.3 reduce-scatter.1

commit v3 on v1

--- a/solution.py
+++ b/solution.py
@@ -1,5 +1,3 @@
-import functools
-
 import jax
 import jax.numpy as jnp
 import numpy as np
@@ -9,9 +7,10 @@
 from jax.sharding import PartitionSpec as P
 
 CAP = 13
-HOT_CAP = 44
 SLOT = 16
 BLOCKS = 4
+NX, NZ = 4, 8
+HOT_ROWS = 48
 MESH = pl.DeviceIdType.MESH
 VMEM = pltpu.VMEM
 BF16 = jnp.bfloat16
@@ -22,11 +21,13 @@
     return jnp.dot(a, b, preferred_element_type=F32)
 
 
-def cold_kernel(
-    tok, pick, mix_hi, mix_lo, pack, unpack, gate_hbm, up_hbm, down_hbm, out,
+def experts_kernel(
+    owner, tok, pick, mix_hi, mix_lo, hot_pick, hot_hi, hot_lo, pack, unpack, gate_hbm, up_hbm, down_hbm, out,
     sent, got, rows, part, relay_up, relay_down, from_up, from_down, spread, back,
     w_gate, w_up, w_down, acc_gate, acc_up,
-    load_sem, disp_send, disp_recv, y_send, y_recv, back_send, back_recv,
+    hot_gate, hot_up, hot_down, half_gate, half_up, half_down, quarter_gate, quarter_up, quarter_down,
+    kept_gate, kept_up, kept_down, piece_gate, piece_up, piece_down, hot_rows, hot_part, hot_got,
+    load_sem, move_send, move_recv, hot_send, hot_recv, disp_send, disp_recv, y_send, y_recv, back_send, back_recv,
 ):
     n_dp, experts = rows.shape[0], got.shape[0] // SLOT
     per = experts // BLOCKS
@@ -37,13 +38,107 @@
     my_block, my_place = mine // per, mine % per
     above, below, across = (me + 1) % n_dp, (me + n_dp - 1) % n_dp, (me + 2) % n_dp
 
-    loads = [
-        pltpu.make_async_copy(src, dst, load_sem.at[i])
-        for i, (src, dst) in enumerate(((gate_hbm, w_gate), (up_hbm, w_up), (down_hbm, w_down)))
-    ]
+    x, z, core = mine // (2 * NZ), (mine // 2) % NZ, mine % 2
+    given, held = (gate_hbm, up_hbm, down_hbm), (w_gate, w_up, w_down)
+    loads = [pltpu.make_async_copy(src, dst, load_sem.at[i]) for i, (src, dst) in enumerate(zip(given, held))]
     for load in loads:
         load.start()
 
+    full, halves = (hot_gate, hot_up, hot_down), (half_gate, half_up, half_down)
+    quarters, kept = (quarter_gate, quarter_up, quarter_down), (kept_gate, kept_up, kept_down)
+    pieces = (piece_gate, piece_up, piece_down)
+    depth, units = w_gate.shape
+    in_half, in_quarter, in_piece = depth // 2, depth // (2 * NX), depth // (2 * NX * NZ)
+
+    def of_full(ref, t, lane, at, size):
+        if t < 2:
+            return ref.at[pl.ds(pl.multiple_of(lane * in_half + at, in_piece), size), :]
+        rows_at = pl.ds(pl.multiple_of(lane * (units // 2), units // 2), units // 2)
+        return ref.at[rows_at, pl.ds(pl.multiple_of(2 * at, 2 * in_piece), 2 * size)]
+
+    def of_half(ref, t, at, size):
+        if t < 2:
+            return ref.at[pl.ds(pl.multiple_of(at, in_piece), size), :]
+        return ref.at[:, pl.ds(pl.multiple_of(2 * at, 2 * in_piece), 2 * size)]
+
+    def move(stage, t, src, dst, to):
+        return pltpu.make_async_remote_copy(
+            src_ref=src, dst_ref=dst, send_sem=move_send.at[stage, t], recv_sem=move_recv.at[stage, t],
+            device_id={"expert": to}, device_id_type=MESH,
+        )
+
+    def moved_amount(stage, t):
+        if stage in (0, 5):
+            return halves[t]
+        return quarters[t].at[pl.ds(0, NX - 1)] if stage in (1, 4) else pieces[t].at[pl.ds(0, NZ - 1)]
+
+    def moved(stage, t, sems=move_recv):
+        amount = moved_amount(stage, t)
+        pltpu.make_async_copy(amount, amount, sems.at[stage, t]).wait()
+
+    twin = mine + 1 - 2 * core
+
+    def along_x(k):
+        to = (x + k) % NX
+        return to, (to * NZ + z) * 2 + core
+
+    def along_z(k):
+        to = (z + k) % NZ
+        return to, (x * NZ + to) * 2 + core
+
+    def swap_halves(t):
+        move(0, t, of_full(given[t], t, 1 - core, 0, in_half), halves[t], twin).start()
+
+    def scatter_x(t):
+        loads[t].wait()
+        moved(0, t)
+
+        @pl.loop(0, 8)
+        def _(i):
+            here = of_half(halves[t], t, i * (in_half // 8), in_half // 8)
+            ours = of_full(held[t], t, core, i * (in_half // 8), in_half // 8)
+            here[...] = jnp.where(owner[2] == core, ours[...], here[...])
+
+        for k in range(1, NX):
+            to, device = along_x(k)
+            move(1, t, of_half(halves[t], t, to * in_quarter, in_quarter), quarters[t].at[x], device).start()
+        quarters[t][x] = of_half(halves[t], t, x * in_quarter, in_quarter)[...]
+
+    def scatter_z(t):
+        moved(1, t)
+        kept[t][...] = quarters[t][owner[0]]
+
+        @pl.loop(1, NZ)
+        def _(k):
+            to, device = along_z(k)
+            move(2, t, of_half(kept[t], t, to * in_piece, in_piece), pieces[t].at[z], device).start()
+
+        pieces[t][z] = of_half(kept[t], t, z * in_piece, in_piece)[...]
+
+    def gather_z(t):
+        moved(2, t)
+        own_piece = of_full(full[t], t, core, x * in_quarter + z * in_piece, in_piece)
+        own_piece[...] = pieces[t][owner[1]]
+
+        @pl.loop(1, NZ)
+        def _(k):
+            move(3, t, own_piece, own_piece, along_z(k)[1]).start()
+
+    def gather_x(t):
+        moved(3, t)
+        own_quarter = of_full(full[t], t, core, x * in_quarter, in_quarter)
+        for k in range(1, NX):
+            move(4, t, own_quarter, own_quarter, along_x(k)[1]).start()
+
+    def join_halves(t):
+        moved(4, t)
+        own_half = of_full(full[t], t, core, 0, in_half)
+        move(5, t, own_half, own_half, twin).start()
+
+    for t in range(3):
+        swap_halves(t)
+
+    hot_at = pl.ds(0, HOT_ROWS)
     own_cols = pl.ds(pl.multiple_of(me * quarter, 128), quarter)
 
     @pl.loop(0, BLOCKS)
@@ -69,6 +164,39 @@
         def _(i, j=j):
             to = ((my_block + j) % BLOCKS) * per + (my_place + i) % per
             exchange(sent, got, to, disp_send, disp_recv.at[j]).start()
+
+    def hot_units():
+        acc_gate[hot_at, :] = jnp.zeros((HOT_ROWS, units), F32)
+        acc_up[hot_at, :] = jnp.zeros((HOT_ROWS, units), F32)
+        moved(5, 0)
+        moved(5, 1)
+
+        @pl.loop(0, n_dp)
+        def _(q):
+            cols = pl.ds(pl.multiple_of(q * quarter, quarter), quarter)
+            inputs = dot(hot_pick[...], tok[:, cols]).astype(BF16)
+            acc_gate[hot_at, :] += dot(inputs, hot_gate[cols, :])
+            acc_up[hot_at, :] += dot(inputs, hot_up[cols, :])
+
+        hot_rows[...] = (jax.nn.silu(acc_gate[hot_at, :]) * acc_up[hot_at, :]).astype(BF16)
+
+    def hot_results():
+        moved(5, 2)
+
+        @pl.loop(0, n_dp)
+        def _(q):
+            cols = pl.ds(pl.multiple_of(q * quarter, quarter), quarter)
+            hot_part[q, :, :] = dot(hot_rows[...], hot_down[:, cols]).astype(BF16)
+
+        for k in range(1, n_dp):
+            hot_copy(k).start()
+
+    def hot_copy(k):
+        to = (me + k) % n_dp
+        return pltpu.make_async_remote_copy(
+            src_ref=hot_part.at[to], dst_ref=hot_got.at[k - 1], send_sem=hot_send.at[k - 1],
+            recv_sem=hot_recv.at[k - 1], device_id={"dp": to}, device_id_type=MESH,
+        )
 
     def across_dp(kind, j, src, dst, to):
         return pltpu.make_async_remote_copy(
@@ -158,33 +286,54 @@
 
     stages = (gather_rows, forward_rows, compute, relay, send_back)
     delays = (0, 1, 2, 3, 4)
-    for step in range(BLOCKS + delays[-1]):
+    moves = (scatter_x, scatter_z, gather_z, gather_x, join_halves)
+    turns = (0, 1, 2, 3, 5)
+    for t in range(3):
+        scatter_x(t)
+    for step in range(max(BLOCKS + delays[-1], 2 + turns[-1])):
         for stage, delay in zip(stages, delays):
-            j = step - delay
-            if 0 <= j < BLOCKS:
-                if stage is compute and j == 0:
-                    for load in loads:
-                        load.wait()
-                stage(j)
+            if 0 <= step - delay < BLOCKS:
+                stage(step - delay)
+        for stage, turn in zip(moves[1:], turns[1:]):
+            t = step + 1 - turn
+            if 0 <= t < 3:
+                stage(t)
+    hot_units()
+    hot_results()
 
     others = pl.ds(0, (experts - 1) * SLOT)
     pltpu.make_async_copy(back.at[others, :], back.at[others, :], back_recv).wait()
     down_rows = (((0,), (0,)), ((), ()))
     mixed = lax.dot_general(mix_hi[...], back[...], down_rows, preferred_element_type=F32)
-    out[...] = mixed + lax.dot_general(mix_lo[...], back[...], down_rows, preferred_element_type=F32)
+    mixed += lax.dot_general(mix_lo[...], back[...], down_rows, preferred_element_type=F32)
+    hot_sum = hot_part[me, :, :].astype(F32)
+    for k in range(1, n_dp):
+        hot_copy(k).wait_recv()
+        hot_sum += hot_got[k - 1, :, :].astype(F32)
+    hot_sum = hot_sum.astype(BF16)
+    mixed += lax.dot_general(hot_hi[...], hot_sum, down_rows, preferred_element_type=F32)
+    mixed += lax.dot_general(hot_lo[...], hot_sum, down_rows, preferred_element_type=F32)
+    out[...] = mixed.astype(BF16)
 
     pltpu.make_async_copy(sent.at[others, :], sent.at[others, :], disp_send).wait()
     pltpu.make_async_copy(spread.at[others, :], spread.at[others, :], back_send).wait()
     for copy in copies.values():
         copy.wait_send()
-
-
-def cold_experts(tokens, pick, mix_hi, mix_lo, w_gate, w_up, w_down):
+    for k in range(1, n_dp):
+        hot_copy(k).wait_send()
+    for t in range(3):
+        for stage in range(6):
+            moved(stage, t, move_send)
+
+
+def routed_experts(owner, tokens, pick, mix_hi, mix_lo, hot_pick, hot_hi, hot_lo, weights):
     group_tok, width = tokens.shape
     experts, n_dp = lax.axis_size("expert"), lax.axis_size("dp")
-    units, quarter, per = w_gate.shape[1], width // n_dp, experts // BLOCKS
+    units, quarter, per = weights[0].shape[1], width // n_dp, experts // BLOCKS
     slots, held = experts * SLOT, experts * CAP
     block = per * CAP
+    kept, kept_down = (width // (2 * NX), units), (units // 2, width // NX)
+    piece, piece_down = (kept[0] // NZ, units), (units // 2, kept_down[1] // NZ)
     place = np.arange(block)
     wanted = (place // CAP) * SLOT + place % CAP
     pack = jnp.asarray(wanted[:, None] == np.arange(per * SLOT)[None, :], BF16)
@@ -192,10 +341,10 @@
     vmem, anywhere = pl.BlockSpec(memory_space=VMEM), pl.BlockSpec(memory_space=pl.ANY)
     dma = pltpu.SemaphoreType.DMA
     return pl.pallas_call(
-        cold_kernel,
-        name="cold_experts",
-        out_shape=jax.ShapeDtypeStruct((group_tok, quarter), F32),
-        in_specs=[vmem] * 6 + [anywhere] * 3,
+        experts_kernel,
+        name="routed_experts",
+        out_shape=jax.ShapeDtypeStruct((group_tok, quarter), BF16),
+        in_specs=[pl.BlockSpec(memory_space=pltpu.SMEM)] + [vmem] * 9 + [anywhere] * 3,
         out_specs=vmem,
         scratch_shapes=[
             VMEM((slots, quarter), BF16),
@@ -213,7 +362,21 @@
             VMEM((units, width), BF16),
             VMEM((block, units), F32),
             VMEM((block, units), F32),
+            VMEM((width, units), BF16),
+            VMEM((width, units), BF16),
+            VMEM((units, width), BF16),
+            *[VMEM(shape, BF16) for shape in ((width // 2, units), (width // 2, units), (units // 2, width))],
+            *[VMEM((NX, *shape), BF16) for shape in (kept, kept, kept_down)],
+            *[VMEM(shape, BF16) for shape in (kept, kept, kept_down)],
+            *[VMEM((NZ, *shape), BF16) for shape in (piece, piece, piece_down)],
+            VMEM((HOT_ROWS, units), BF16),
+            VMEM((n_dp, HOT_ROWS, quarter), BF16),
+            VMEM((n_dp - 1, HOT_ROWS, quarter), BF16),
             dma((3,)),
+            dma((6, 3)),
+            dma((6, 3)),
+            dma((n_dp - 1,)),
+            dma((n_dp - 1,)),
             dma,
             dma((BLOCKS,)),
             dma((8, BLOCKS)),
@@ -221,18 +384,11 @@
             dma,
             dma,
         ],
-        compiler_params=pltpu.CompilerParams(vmem_limit_bytes=56 << 20, has_side_effects=True),
+        compiler_params=pltpu.CompilerParams(vmem_limit_bytes=63 << 20, has_side_effects=True),
         cost_estimate=pl.CostEstimate(
             flops=6 * held * width * units, bytes_accessed=60 << 20, transcendentals=held * units
         ),
-    )(tokens, pick, mix_hi, mix_lo, pack, unpack, w_gate, w_up, w_down)
-
-
-def expert_partial(inputs, gate_mat, up_mat, down_mat):
-    gate_val = jnp.dot(inputs, gate_mat, preferred_element_type=F32)
-    up_val = jnp.dot(inputs, up_mat, preferred_element_type=F32)
-    hidden = (jax.nn.silu(gate_val) * up_val).astype(BF16)
-    return jnp.dot(hidden, down_mat, preferred_element_type=F32)
+    )(owner, tokens, pick, mix_hi, mix_lo, hot_pick, hot_hi, hot_lo, pack, unpack, *weights)
 
 
 def split_weight(weight):
@@ -264,22 +420,16 @@
 
     hot_rank = jnp.sum(jnp.where(is_hot, rank, 0.0), axis=0)
     hot_weight = jnp.sum(jnp.where(is_hot, weight, 0.0), axis=0)
-    hot_pick = hot_rank[None, :] == jnp.arange(HOT_CAP, dtype=F32)[:, None]
-
-    owned = lax.axis_index("expert") == hot_expert
-    hot_gate, hot_up, hot_down = lax.psum(
-        tuple(jnp.where(owned, w, jnp.zeros_like(w)) for w in (w_gate, w_up, w_down)), "expert"
-    )
-    cold = cold_experts(group_rows, pick, mix_hi, mix_lo, w_gate, w_up, w_down)
-    hot_rows = jnp.dot(hot_pick.astype(BF16), group_rows, preferred_element_type=F32).astype(BF16)
-    hot_part = expert_partial(hot_rows, hot_gate, hot_up, hot_down)
-    hot_sum = lax.psum_scatter(hot_part.astype(BF16), "dp", scatter_dimension=1, tiled=True)
-    hot_mix = jnp.where(hot_pick, hot_weight[None, :], 0.0)
-    hot = lax.dot_general(
-        hot_mix, hot_sum.astype(F32), (((0,), (0,)), ((), ())),
-        precision=lax.Precision.HIGHEST, preferred_element_type=F32,
-    )
-    return (cold + hot).astype(BF16)[None]
+    hot_picked = hot_rank[None, :] == jnp.arange(HOT_ROWS, dtype=F32)[:, None]
+    hot_high, hot_low = split_weight(hot_weight)
+    hot_pick = hot_picked.astype(BF16)
+    hot_hi = jnp.where(hot_picked, hot_high[None, :], zero)
+    hot_lo = jnp.where(hot_picked, hot_low[None, :], zero)
+
+    weights = (w_gate, w_up, w_down)
+    owner = jnp.stack([hot_expert // (2 * NZ), (hot_expert // 2) % NZ, hot_expert % 2])
+    mixed = routed_experts(owner, group_rows, pick, mix_hi, mix_lo, hot_pick, hot_hi, hot_lo, weights)
+    return mixed[None]
 
 
 def solution(mesh):

time: 411 us -> 203 us (0.49)
  waiting for transfers between devices: 207 us -> 0 us
  Pallas kernels: 167 us -> 191 us
  between operations: 14.1 us -> 2.83 us
  matrix products: 9.8 us -> 0.89 us
  other arithmetic: 11.6 us -> 6.38 us
    psum x1 -> x0, waiting for transfers between devices: 207 us -> none  [local(): lax.psum(tuple((jnp.where(owned, w, jnp.zeros_like(w)) for w in (w_gate,...]
    pallas_call x1, Pallas kernels: 167 us -> 191 us  [routed_experts(): pl.pallas_call(experts_kernel, name='routed_experts', out_shape=jax.Shape...]
    dot_general x4 -> x0, matrix products: 9.65 us -> none  [the longest x1 4.07 us: expert_partial(): return jnp.dot(hidden, down_mat, preferred_element_type=F32)]
    select_n x2 -> x1, other arithmetic: 7.09 us -> 0.62 us  [local(): hot_lo = jnp.where(hot_picked, hot_low[None, :], zero)]
  transfers between devices with their start and end apart: 2 -> 0, of which waited for: 1 -> 0; matrix products, arithmetic and copies ran while one was open for 1% -> 0% of each run, Pallas kernels for 41% -> 0%
where the time goes in v3:
time: 203 us; the launch traced here: 202 us
  Pallas kernels  191 us (94%)
  other arithmetic  6.38 us (3%)
  between operations  2.83 us (1%)
    pallas_call x1, Pallas kernels, routed_experts(): pl.pallas_call(experts_kernel, name='routed_experts', out_shape=jax.Shape...  191 us

profile of v3, /device:TPU:1, one launch (start us, length us, event | category | flops | bytes accessed | tf_op | source)
XLA Modules:
  0.0 202.4 jit_solution(3728753174888837425)
XLA Ops:
  0.0 0.1 eq.71
  0.1 1.3 select_reduce_fusion
  1.4 0.7 iota_reduce_fusion
  4.9 0.6 pad_add_fusion.owner
  5.5 0.7 iota_compare_fusion.2
  6.2 0.9 select_reduce_fusion.1
  7.1 0.6 fusion.6.hot_pick
  7.7 0.6 fusion.4
  8.3 0.9 fusion.2.pick
  9.2 1.0 fusion
  10.2 190.6 %routed_experts.1 = bf16[88,1024]{1,0:T(8,128)(2,1)} custom-call(s32[3]{0:T(128)} %pad_add_fusion.owner, bf16[88,4096]{1,0:T(8,128)(2,1)} %bitcast.33, bf16[1024,88]{1,0:T(8,128)(2,1)} %fusion.2.pick, bf16[1024,88]{1,0:T(8,128)(2,1)} %get-tuple-element.13.mix_hi, bf16[1024,88]{1,0:T(8,128)(2,1)} %get-tuple-element.12.mix_lo, bf16[48,88]{1,0:T(8,128)(2,1)} %fusion.6.hot_pick, ...), custom_call_target="tpu_custom_call" | custom-call | flops 7851737088 | bytes 62914560 | tf_op jit(solution)/shard_map/routed_experts/pallas_call | solution.py:343
  200.8 1.6 copy.11
  (2 shorter events, 0.0 us)

commit v4 on v3

--- a/solution.py
+++ b/solution.py
@@ -22,7 +22,8 @@
 
 
 def experts_kernel(
-    owner, tok, pick, mix_hi, mix_lo, hot_pick, hot_hi, hot_lo, pack, unpack, gate_hbm, up_hbm, down_hbm, out,
+    tok, chosen, mixing, pack, unpack, gate_hbm, up_hbm, down_hbm, out,
+    mix_hi, mix_lo, hot_pick, hot_hi, hot_lo,
     sent, got, rows, part, relay_up, relay_down, from_up, from_down, spread, back,
     w_gate, w_up, w_down, acc_gate, acc_up,
     hot_gate, hot_up, hot_down, half_gate, half_up, half_down, quarter_gate, quarter_up, quarter_down,
@@ -38,6 +39,15 @@
     my_block, my_place = mine // per, mine % per
     above, below, across = (me + 1) % n_dp, (me + n_dp - 1) % n_dp, (me + 2) % n_dp
 
+    barrier = pltpu.get_barrier_semaphore()
+
+    @pl.loop(1, experts)
+    def _(k):
+        pl.semaphore_signal(barrier, inc=1, device_id={"expert": (mine + k) % experts}, device_id_type=MESH)
+
+    for k in range(1, n_dp):
+        pl.semaphore_signal(barrier, inc=1, device_id={"dp": (me + k) % n_dp}, device_id_type=MESH)
+
     x, z, core = mine // (2 * NZ), (mine // 2) % NZ, mine % 2
     given, held = (gate_hbm, up_hbm, down_hbm), (w_gate, w_up, w_down)
     loads = [pltpu.make_async_copy(src, dst, load_sem.at[i]) for i, (src, dst) in enumerate(zip(given, held))]
@@ -97,7 +107,7 @@
         def _(i):
             here = of_half(halves[t], t, i * (in_half // 8), in_half // 8)
             ours = of_full(held[t], t, core, i * (in_half // 8), in_half // 8)
-            here[...] = jnp.where(owner[2] == core, ours[...], here[...])
+            here[...] = ours[...] * matches(owner_core, core) + here[...] * matches(owner_core, 1 - core)
 
         for k in range(1, NX):
             to, device = along_x(k)
@@ -106,7 +116,7 @@
 
     def scatter_z(t):
         moved(1, t)
-        kept[t][...] = quarters[t][owner[0]]
+        kept[t][...] = sum(quarters[t][i] * matches(owner_x, i) for i in range(NX))
 
         @pl.loop(1, NZ)
         def _(k):
@@ -118,7 +128,7 @@
     def gather_z(t):
         moved(2, t)
         own_piece = of_full(full[t], t, core, x * in_quarter + z * in_piece, in_piece)
-        own_piece[...] = pieces[t][owner[1]]
+        own_piece[...] = sum(pieces[t][i] * matches(owner_z, i) for i in range(NZ))
 
         @pl.loop(1, NZ)
         def _(k):
@@ -135,16 +145,79 @@
         own_half = of_full(full[t], t, core, 0, in_half)
         move(5, t, own_half, own_half, twin).start()
 
-    for t in range(3):
-        swap_halves(t)
-
     hot_at = pl.ds(0, HOT_ROWS)
     own_cols = pl.ds(pl.multiple_of(me * quarter, 128), quarter)
+    group_tok, top = chosen.shape
+    first_rows = (((0,), (0,)), ((), ()))
+
+    def count(shape, axis):
+        return lax.broadcasted_iota(jnp.int32, shape, axis)
+
+    def as_ones(mask):
+        return jnp.where(mask, 1.0, 0.0).astype(BF16)
+
+    def turned(value):
+        size = value.shape[0]
+        eye = as_ones(count((size, size), 0) == count((size, size), 1))
+        return lax.dot_general(value.astype(BF16), eye, first_rows, preferred_element_type=F32)
+
+    high = mixing[...].astype(BF16)
+    low = (mixing[...] - high.astype(F32)).astype(BF16)
+    ids, high, low = turned(chosen[...].astype(F32)), turned(high), turned(low)
+    expert = count((experts, group_tok), 0).astype(F32)
+    member, weight_hi, weight_lo = (jnp.zeros((experts, group_tok), F32) for _ in range(3))
+    for k in range(top):
+        hit = ids[k : k + 1, :] == expert
+        member += jnp.where(hit, 1.0, 0.0)
+        weight_hi += jnp.where(hit, high[k : k + 1, :], 0.0)
+        weight_lo += jnp.where(hit, low[k : k + 1, :], 0.0)
+    earlier = as_ones(count((group_tok, group_tok), 0) < count((group_tok, group_tok), 1))
+    rank = jnp.where(member > 0.0, dot(member.astype(BF16), earlier), -1.0)
+    picks = jnp.sum(member, axis=1, keepdims=True)
+    is_hot = picks == jnp.max(picks, axis=0, keepdims=True)
+    cold_rank = jnp.where(is_hot, -1.0, rank)
+
+    def of_hot(value):
+        return jnp.sum(jnp.where(is_hot, value, 0.0), axis=0, keepdims=True)
+
+    place = count((experts, 1), 0)
+    z_bits = NZ.bit_length() - 1
+    owner_core = of_hot((place & 1).astype(F32))
+    owner_z = of_hot((lax.shift_right_logical(place, 1) & (NZ - 1)).astype(F32))
+    owner_x = of_hot(lax.shift_right_logical(place, 1 + z_bits).astype(F32))
+
+    def matches(value, index):
+        return as_ones(value == jnp.asarray(index).astype(F32))
+
+    hot_picked = of_hot(rank) == count((HOT_ROWS, group_tok), 0).astype(F32)
+    hot_pick[...] = as_ones(hot_picked)
+    hot_hi[...] = jnp.where(hot_picked, of_hot(weight_hi), 0.0).astype(BF16)
+    hot_lo[...] = jnp.where(hot_picked, of_hot(weight_lo), 0.0).astype(BF16)
+
+    def belongs(slot_at, expert_at):
+        return as_ones(jnp.logical_and(slot_at >= expert_at * SLOT, slot_at < (expert_at + 1) * SLOT))
 
     @pl.loop(0, BLOCKS)
     def _(b):
         at = pl.ds(pl.multiple_of(b * padded, padded), padded)
-        sent[at, :] = dot(pick[at, :], tok[:, own_cols]).astype(BF16)
+        spread_out = belongs(count((padded, experts), 0) + b * padded, count((padded, experts), 1))
+        slots = (count((padded, group_tok), 0) & (SLOT - 1)).astype(F32)
+        pick = as_ones(dot(spread_out, cold_rank.astype(BF16)) == slots)
+        sent[at, :] = dot(pick, tok[:, own_cols]).astype(BF16)
+
+    def mixing_tables():
+        by_token = [turned(value).astype(BF16) for value in (cold_rank, weight_hi, weight_lo)]
+
+        @pl.loop(0, BLOCKS)
+        def _(b):
+            at = pl.ds(pl.multiple_of(b * padded, padded), padded)
+            spread_out = belongs(count((experts, padded), 1) + b * padded, count((experts, padded), 0))
+            slots = (count((group_tok, padded), 1) & (SLOT - 1)).astype(F32)
+            picked = dot(by_token[0], spread_out) == slots
+            mix_hi[:, at] = jnp.where(picked, dot(by_token[1], spread_out), 0.0).astype(BF16)
+            mix_lo[:, at] = jnp.where(picked, dot(by_token[2], spread_out), 0.0).astype(BF16)
+
+    pl.semaphore_wait(barrier, experts - 1 + n_dp - 1)
 
     def slot(i):
         return pl.ds(pl.multiple_of(i * SLOT, SLOT), SLOT)
@@ -164,6 +237,10 @@
         def _(i, j=j):
             to = ((my_block + j) % BLOCKS) * per + (my_place + i) % per
             exchange(sent, got, to, disp_send, disp_recv.at[j]).start()
+
+    for t in range(3):
+        swap_halves(t)
+    mixing_tables()
 
     def hot_units():
         acc_gate[hot_at, :] = jnp.zeros((HOT_ROWS, units), F32)
@@ -303,16 +380,14 @@
 
     others = pl.ds(0, (experts - 1) * SLOT)
     pltpu.make_async_copy(back.at[others, :], back.at[others, :], back_recv).wait()
-    down_rows = (((0,), (0,)), ((), ()))
-    mixed = lax.dot_general(mix_hi[...], back[...], down_rows, preferred_element_type=F32)
-    mixed += lax.dot_general(mix_lo[...], back[...], down_rows, preferred_element_type=F32)
+    mixed = dot(mix_hi[...], back[...]) + dot(mix_lo[...], back[...])
     hot_sum = hot_part[me, :, :].astype(F32)
     for k in range(1, n_dp):
         hot_copy(k).wait_recv()
         hot_sum += hot_got[k - 1, :, :].astype(F32)
     hot_sum = hot_sum.astype(BF16)
-    mixed += lax.dot_general(hot_hi[...], hot_sum, down_rows, preferred_element_type=F32)
-    mixed += lax.dot_general(hot_lo[...], hot_sum, down_rows, preferred_element_type=F32)
+    mixed += lax.dot_general(hot_hi[...], hot_sum, first_rows, preferred_element_type=F32)
+    mixed += lax.dot_general(hot_lo[...], hot_sum, first_rows, preferred_element_type=F32)
     out[...] = mixed.astype(BF16)
 
     pltpu.make_async_copy(sent.at[others, :], sent.at[others, :], disp_send).wait()
@@ -326,7 +401,9 @@
             moved(stage, t, move_send)
 
 
-def routed_experts(owner, tokens, pick, mix_hi, mix_lo, hot_pick, hot_hi, hot_lo, weights):
+def local(tokens, routing, combine, *weights):
+    tokens, routing, combine = tokens[0], routing[0], combine[0]
+    weights = [weight[0] for weight in weights]
     group_tok, width = tokens.shape
     experts, n_dp = lax.axis_size("expert"), lax.axis_size("dp")
     units, quarter, per = weights[0].shape[1], width // n_dp, experts // BLOCKS
@@ -340,13 +417,16 @@
     unpack = jnp.asarray(wanted[None, :] == np.arange(per * SLOT)[:, None], BF16)
     vmem, anywhere = pl.BlockSpec(memory_space=VMEM), pl.BlockSpec(memory_space=pl.ANY)
     dma = pltpu.SemaphoreType.DMA
-    return pl.pallas_call(
+    mixed = pl.pallas_call(
         experts_kernel,
         name="routed_experts",
         out_shape=jax.ShapeDtypeStruct((group_tok, quarter), BF16),
-        in_specs=[pl.BlockSpec(memory_space=pltpu.SMEM)] + [vmem] * 9 + [anywhere] * 3,
+        in_specs=[vmem] * 5 + [anywhere] * 3,
         out_specs=vmem,
         scratch_shapes=[
+            VMEM((group_tok, slots), BF16),
+            VMEM((group_tok, slots), BF16),
+            *[VMEM((HOT_ROWS, group_tok), BF16)] * 3,
             VMEM((slots, quarter), BF16),
             VMEM((slots, quarter), BF16),
             VMEM((n_dp, held, quarter), BF16),
@@ -384,51 +464,11 @@
             dma,
             dma,
         ],
-        compiler_params=pltpu.CompilerParams(vmem_limit_bytes=63 << 20, has_side_effects=True),
+        compiler_params=pltpu.CompilerParams(vmem_limit_bytes=63 << 20, has_side_effects=True, collective_id=0),
         cost_estimate=pl.CostEstimate(
             flops=6 * held * width * units, bytes_accessed=60 << 20, transcendentals=held * units
         ),
-    )(owner, tokens, pick, mix_hi, mix_lo, hot_pick, hot_hi, hot_lo, pack, unpack, *weights)
-
-
-def split_weight(weight):
-    high = lax.reduce_precision(weight, 8, 7)
-    return high.astype(BF16), (weight - high).astype(BF16)
-
-
-def local(tokens, routing, combine, w_gate, w_up, w_down):
-    group_rows, chosen, mixing = tokens[0], routing[0], combine[0]
-    w_gate, w_up, w_down = w_gate[0], w_up[0], w_down[0]
-    group_tok = chosen.shape[0]
-    experts = lax.axis_size("expert")
-    ids = jnp.arange(experts, dtype=jnp.int32)
-    hit = chosen.T[None, :, :] == ids[:, None, None]
-    member = jnp.sum(hit.astype(F32), axis=1)
-    weight = jnp.sum(jnp.where(hit, mixing.T[None, :, :], 0.0), axis=1)
-    earlier = jnp.asarray(np.triu(np.ones((group_tok, group_tok)), 1), BF16)
-    before = jnp.dot(member.astype(BF16), earlier, preferred_element_type=F32)
-    hot_expert = jnp.argmax(jnp.sum(member, axis=1)).astype(jnp.int32)
-    is_hot = (ids == hot_expert)[:, None]
-    rank = jnp.where(member > 0, before, -1.0)
-
-    picked = jnp.where(is_hot, -1.0, rank)[:, None, :] == jnp.arange(SLOT, dtype=F32)[None, :, None]
-    high, low = split_weight(weight)
-    zero = jnp.zeros((), BF16)
-    pick = picked.astype(BF16).reshape(experts * SLOT, group_tok)
-    mix_hi = jnp.where(picked, high[:, None, :], zero).reshape(experts * SLOT, group_tok)
-    mix_lo = jnp.where(picked, low[:, None, :], zero).reshape(experts * SLOT, group_tok)
-
-    hot_rank = jnp.sum(jnp.where(is_hot, rank, 0.0), axis=0)
-    hot_weight = jnp.sum(jnp.where(is_hot, weight, 0.0), axis=0)
-    hot_picked = hot_rank[None, :] == jnp.arange(HOT_ROWS, dtype=F32)[:, None]
-    hot_high, hot_low = split_weight(hot_weight)
-    hot_pick = hot_picked.astype(BF16)
-    hot_hi = jnp.where(hot_picked, hot_high[None, :], zero)
-    hot_lo = jnp.where(hot_picked, hot_low[None, :], zero)
-
-    weights = (w_gate, w_up, w_down)
-    owner = jnp.stack([hot_expert // (2 * NZ), (hot_expert // 2) % NZ, hot_expert % 2])
-    mixed = routed_experts(owner, group_rows, pick, mix_hi, mix_lo, hot_pick, hot_hi, hot_lo, weights)
+    )(tokens, routing, combine, pack, unpack, *weights)
     return mixed[None]
 
 

time: 203 us -> 188 us (0.926)
  Pallas kernels: 191 us -> 183 us
  other arithmetic: 6.38 us -> 0 us
  between operations: 2.83 us -> 0.01 us
  local copies, waits for them, and re-layouts: 1.69 us -> 4.39 us
    pallas_call x1, Pallas kernels: 191 us -> 183 us  [local(): pl.pallas_call(experts_kernel, name='routed_experts', out_shape=jax.Shape...]
    unnamed x1 -> x3, local copies, waits for them, and re-layouts: 1.61 us -> 4.39 us
where the time goes in v4:
time: 188 us; the launch traced here: 187 us
  Pallas kernels  183 us (97%)
  local copies, waits for them, and re-layouts  4.39 us (2%)
    pallas_call x1, Pallas kernels, local(): pl.pallas_call(experts_kernel, name='routed_experts', out_shape=jax.Shape...  183 us
    unnamed x3, local copies, waits for them, and re-layouts  4.39 us

profile of v4, /device:TPU:1, one launch (start us, length us, event | category | flops | bytes accessed | tf_op | source)
XLA Modules:
  0.0 187.3 jit_solution(10841058607867340912)
XLA Ops:
  0.0 1.4 copy.9
  1.4 1.4 copy.10
  2.8 182.9 %routed_experts.1 = bf16[88,1024]{1,0:T(8,128)(2,1)} custom-call(bf16[88,4096]{1,0:T(8,128)(2,1)} %bitcast.13, s32[88,8]{1,0:T(8,128)} %bitcast.8, f32[88,8]{1,0:T(8,128)} %bitcast.9, bf16[208,256]{1,0:T(8,128)(2,1)} %constant.4.clone.pack, bf16[256,208]{1,0:T(8,128)(2,1)} %constant.5.clone.unpack, bf16[4096,384]{1,0:T(8,128)(2,1)} %bitcast.10, ...), custom_call_target="tpu_custom_call" | custom-call | flops 7851737088 | bytes 62914560 | tf_op jit(solution)/shard_map/routed_experts/pallas_call | solution.py:420
  185.7 1.6 copy.12

commit v5 on v4

--- a/solution.py
+++ b/solution.py
@@ -147,7 +147,7 @@
 
     hot_at = pl.ds(0, HOT_ROWS)
     own_cols = pl.ds(pl.multiple_of(me * quarter, 128), quarter)
-    group_tok, top = chosen.shape
+    top, group_tok = chosen.shape
     first_rows = (((0,), (0,)), ((), ()))
 
     def count(shape, axis):
@@ -163,7 +163,7 @@
 
     high = mixing[...].astype(BF16)
     low = (mixing[...] - high.astype(F32)).astype(BF16)
-    ids, high, low = turned(chosen[...].astype(F32)), turned(high), turned(low)
+    ids, high, low = chosen[...].astype(F32), high.astype(F32), low.astype(F32)
     expert = count((experts, group_tok), 0).astype(F32)
     member, weight_hi, weight_lo = (jnp.zeros((experts, group_tok), F32) for _ in range(3))
     for k in range(top):
@@ -402,7 +402,7 @@
 
 
 def local(tokens, routing, combine, *weights):
-    tokens, routing, combine = tokens[0], routing[0], combine[0]
+    tokens, routing, combine = tokens[0], routing[0].T, combine[0].T
     weights = [weight[0] for weight in weights]
     group_tok, width = tokens.shape
     experts, n_dp = lax.axis_size("expert"), lax.axis_size("dp")

time: 188 us -> 185 us (0.984)
  local copies, waits for them, and re-layouts: 4.39 us -> 1.61 us
    unnamed x3 -> x1, local copies, waits for them, and re-layouts: 4.39 us -> 1.61 us
where the time goes in v5:
time: 185 us
  Pallas kernels  183 us (99%)
    pallas_call x1, Pallas kernels, local(): pl.pallas_call(experts_kernel, name='routed_experts', out_shape=jax.Shape...  183 us

profile of v5, /device:TPU:1, one launch (start us, length us, event | category | flops | bytes accessed | tf_op | source)
XLA Modules:
  0.0 184.5 jit_solution(1430758503875835008)
XLA Ops:
  0.0 182.9 %routed_experts.1 = bf16[88,1024]{1,0:T(8,128)(2,1)} custom-call(bf16[88,4096]{1,0:T(8,128)(2,1)} %bitcast.15, s32[8,88]{1,0:T(8,128)} %bitcast.16, f32[8,88]{1,0:T(8,128)} %bitcast.17, bf16[208,256]{1,0:T(8,128)(2,1)} %constant.4.clone.pack, bf16[256,208]{1,0:T(8,128)(2,1)} %constant.5.clone.unpack, bf16[4096,384]{1,0:T(8,128)(2,1)} %bitcast.12, ...), custom_call_target="tpu_custom_call" | custom-call | flops 7851737088 | bytes 62914560 | tf_op jit(solution)/shard_map/routed_experts/pallas_call | solution.py:420
  182.9 1.6 copy.10

commit v6 on v5

--- a/solution.py
+++ b/solution.py
@@ -231,6 +231,9 @@
             device_id={"expert": to}, device_id_type=MESH,
         )
 
+    for t in range(3):
+        swap_halves(t)
+
     for j in range(BLOCKS):
 
         @pl.loop(1 if j == 0 else 0, per)
@@ -238,8 +241,6 @@
             to = ((my_block + j) % BLOCKS) * per + (my_place + i) % per
             exchange(sent, got, to, disp_send, disp_recv.at[j]).start()
 
-    for t in range(3):
-        swap_halves(t)
     mixing_tables()
 
     def hot_units():
@@ -365,13 +366,12 @@
     delays = (0, 1, 2, 3, 4)
     moves = (scatter_x, scatter_z, gather_z, gather_x, join_halves)
     turns = (0, 1, 2, 3, 5)
-    for t in range(3):
-        scatter_x(t)
+    scatter_x(0)
     for step in range(max(BLOCKS + delays[-1], 2 + turns[-1])):
         for stage, delay in zip(stages, delays):
             if 0 <= step - delay < BLOCKS:
                 stage(step - delay)
-        for stage, turn in zip(moves[1:], turns[1:]):
+        for stage, turn in zip(moves, turns):
             t = step + 1 - turn
             if 0 <= t < 3:
                 stage(t)

time: 185 us -> 184 us (level)
  no operation moved by 1% of the time
where the time goes in v6:
time: 184 us
  Pallas kernels  182 us (99%)
    pallas_call x1, Pallas kernels, local(): pl.pallas_call(experts_kernel, name='routed_experts', out_shape=jax.Shape...  182 us

profile of v6, /device:TPU:1, one launch (start us, length us, event | category | flops | bytes accessed | tf_op | source)
XLA Modules:
  0.0 183.8 jit_solution(16700661783068193748)
XLA Ops:
  0.0 182.2 %routed_experts.1 = bf16[88,1024]{1,0:T(8,128)(2,1)} custom-call(bf16[88,4096]{1,0:T(8,128)(2,1)} %bitcast.15, s32[8,88]{1,0:T(8,128)} %bitcast.16, f32[8,88]{1,0:T(8,128)} %bitcast.17, bf16[208,256]{1,0:T(8,128)(2,1)} %constant.4.clone.pack, bf16[256,208]{1,0:T(8,128)(2,1)} %constant.5.clone.unpack, bf16[4096,384]{1,0:T(8,128)(2,1)} %bitcast.12, ...), custom_call_target="tpu_custom_call" | custom-call | flops 7851737088 | bytes 62914560 | tf_op jit(solution)/shard_map/routed_experts/pallas_call | solution.py:420
  182.2 1.6 copy.10
